TPU v7x, 32 devices: a whole 2x2x4 slice. The times are simulated.
32 devices in a mesh: dp: 8 (over z, y), seq: 4 (over x, core).
Axes of the slice: x: 2, y: 2, z: 4, core: 2. Of those that a mesh axis runs over, the one named last changes fastest.
Arguments:
- tokens: bfloat16 [8192, 768], P(('dp', 'seq')), may hold values from -6 to 6
- ln1_gain: bfloat16 [768], P('dp'), may hold values from 0.25 to 1.75
- w_qkv: bfloat16 [768, 2304], P('dp'), may hold values from -0.21875 to 0.21875
- w_out: bfloat16 [768, 768], P('dp'), may hold values from -1.75 to 1.75
- w_ada: bfloat16 [768, 2304], P('dp'), may hold values from -0.21875 to 0.21875
- w_up: bfloat16 [768, 3072], P('dp'), may hold values from -0.21875 to 0.21875
- w_down: bfloat16 [3072, 768], P('dp'), may hold values from -0.109375 to 0.109375
- out_grad: bfloat16 [8192, 768], P(('dp', 'seq')), may hold values from -6 to 6
- layout: int32 [8, 2], P('dp'), may hold values from 256 to 896, as said below
- timestep: int32 [8], P('dp'), may hold values from 0 to 999
Outputs:
- layer_out: bfloat16 [8192, 768], P(('dp', 'seq'))
- input_grad: bfloat16 [8192, 768], P(('dp', 'seq'))
- gain_grad: float32 [768], P('dp')
- qkv_weight_grad: float32 [768, 2304], P('dp')
- out_weight_grad: float32 [768, 768], P('dp')
- ada_weight_grad: float32 [768, 2304], P('dp')
- up_weight_grad: float32 [768, 3072], P('dp')
- down_weight_grad: float32 [3072, 768], P('dp')
Inputs may be any that keep to these rules, and one draw needn't show every extreme that they name: layout[g] = (P, C): tokens below P are the prompt, the first continuation runs from P to C - 1, the second from C to 1023; P lies between 256 and 512, and each continuation holds at least a quarter of the tokens after the prompt.
All inputs are finite; a program needn't handle non-finite values.
Results may differ from a plain program's by a relative error of at most 0.017.
Values may be sent and summed in bfloat16 or wider, within the bound.
No kernel may reach another device: no remote copies, remote signals or barrier semaphores. Data moves between devices by JAX's collectives and lax.ppermute only.
A program may use at most 128 MiB of HBM per device.

v0:
```python
import math
import jax
import jax.numpy as jnp
from jax import lax
from jax.sharding import PartitionSpec as P

HEADS = 12
HEAD_DIM = 64
eps = 1e-05
neg_fill = -1e30


def layer_norm(values_in):
    average = jnp.mean(values_in, axis=-1, keepdims=True)
    centred = values_in - average
    variance = jnp.mean(centred * centred, axis=-1, keepdims=True)
    scaling = lax.rsqrt(variance + eps)
    return (centred * scaling, scaling)


def norm_back(grad_normed, normed, scaling):
    first_mean = jnp.mean(grad_normed, axis=-1, keepdims=True)
    second_mean = jnp.mean(grad_normed * normed, axis=-1, keepdims=True)
    return scaling * (grad_normed - first_mean - normed * second_mean)


def rope_tables(positions):
    half_dim = HEAD_DIM // 2
    frequency = jnp.exp(
        -math.log(10000.0) * 2.0 * jnp.arange(half_dim, dtype=jnp.float32) / HEAD_DIM
    )
    angles = positions.astype(jnp.float32)[:, None] * frequency[None, :]
    return (jnp.cos(angles), jnp.sin(angles))


def rotate(values_in, cos_table, sine_table, direction):
    half_dim = HEAD_DIM // 2
    front_half = values_in[..., :half_dim]
    back_half = values_in[..., half_dim:]
    cos_part = cos_table[:, None, :]
    sine_part = sine_table[:, None, :] * direction
    return jnp.concatenate(
        [
            front_half * cos_part - back_half * sine_part,
            back_half * cos_part + front_half * sine_part,
        ],
        axis=-1,
    )


def visible(query_pos, key_pos, prompt_end, second_start):
    query_segment = (query_pos >= prompt_end).astype(jnp.int32) + (
        query_pos >= second_start
    ).astype(jnp.int32)
    key_segment = (key_pos >= prompt_end).astype(jnp.int32) + (key_pos >= second_start).astype(
        jnp.int32
    )
    return (key_pos[None, :] < prompt_end) | (query_segment[:, None] == key_segment[None, :])


def time_table(time_steps, model_width):
    half_dim = model_width // 2
    frequency = jnp.exp(-math.log(10000.0) * jnp.arange(half_dim, dtype=jnp.float32) / half_dim)
    angles = time_steps[:, None] * frequency[None, :]
    return jnp.concatenate([jnp.cos(angles), jnp.sin(angles)], axis=1)


def left_product(left, right):
    return lax.dot_general(
        left, right, (((0,), (0,)), ((), ())), preferred_element_type=jnp.float32
    )


def right_product(left, right):
    return lax.dot_general(
        left, right, (((1,), (1,)), ((), ())), preferred_element_type=jnp.float32
    )


def split_rows(grad_full, data_count):
    return grad_full.reshape(data_count, grad_full.shape[0] // data_count, -1)


def body(tokens, ln1_gain, w_qkv, w_out, w_ada, w_up, w_down, out_grad, layout, timestep):
    seq_count = lax.axis_size("seq")
    seq_rank = lax.axis_index("seq")
    tok_rows = tokens.shape[0]
    model_width = tokens.shape[1]
    group_rows = tok_rows * seq_count
    heads_local = HEADS // seq_count
    local_width = heads_local * HEAD_DIM
    block_rows = min(512, group_rows)
    blocks = group_rows // block_rows
    gain_full, qkv_weight, out_weight = (
        lax.all_gather(ln1_gain, "dp", axis=0, tiled=True),
        lax.all_gather(w_qkv, "dp", axis=0, tiled=True),
        lax.all_gather(w_out, "dp", axis=0, tiled=True),
    )
    ada_weight, up_weight, down_weight = (
        lax.all_gather(w_ada, "dp", axis=0, tiled=True),
        lax.all_gather(w_up, "dp", axis=0, tiled=True),
        lax.all_gather(w_down, "dp", axis=0, tiled=True),
    )
    gain_float = gain_full.astype(jnp.float32)
    inputs = tokens.astype(jnp.float32)
    normed_one, scaling_one = layer_norm(inputs)
    hidden_one = (normed_one * gain_float).astype(jnp.bfloat16)
    projected = jnp.dot(hidden_one, qkv_weight, preferred_element_type=jnp.float32).reshape(
        tok_rows, 3, HEADS, HEAD_DIM
    )
    positions = seq_rank * tok_rows + jnp.arange(tok_rows, dtype=jnp.int32)
    cos_table, sine_table = rope_tables(positions)
    rotated = jnp.stack(
        [
            rotate(projected[:, 0], cos_table, sine_table, 1.0),
            rotate(projected[:, 1], cos_table, sine_table, 1.0),
            projected[:, 2],
        ],
        axis=1,
    )
    outgoing = rotated.astype(jnp.bfloat16).reshape(tok_rows, 3, seq_count, local_width)
    incoming = lax.all_to_all(outgoing, "seq", split_axis=2, concat_axis=0, tiled=True).reshape(
        group_rows, 3, heads_local, HEAD_DIM
    )
    queries = incoming[:, 0]
    keys_all = incoming[:, 1]
    values_all = incoming[:, 2]
    prompt_end = layout[0, 0]
    second_start = layout[0, 1]
    key_pos = jnp.arange(group_rows, dtype=jnp.int32)

    def scores_of(query_block, start):
        raw_scores = (
            jnp.einsum("qhd,khd->hqk", query_block, keys_all, preferred_element_type=jnp.float32)
            * 0.125
        )
        query_pos = start + jnp.arange(block_rows, dtype=jnp.int32)
        allowed = visible(query_pos, key_pos, prompt_end, second_start)
        return jnp.where(allowed[None], raw_scores, neg_fill)

    query_blocks = queries.reshape(blocks, block_rows, heads_local, HEAD_DIM)
    starts = jnp.arange(blocks, dtype=jnp.int32) * block_rows

    def forward_block(operands):
        query_block, start = operands
        scores = scores_of(query_block, start)
        row_max = jnp.max(scores, axis=-1, keepdims=True)
        exponent = jnp.exp(scores - row_max)
        row_sum = jnp.sum(exponent, axis=-1, keepdims=True)
        attn_probs = (exponent / row_sum).astype(jnp.bfloat16)
        block_out = jnp.einsum(
            "hqk,khd->qhd", attn_probs, values_all, preferred_element_type=jnp.float32
        )
        return (block_out.astype(jnp.bfloat16), (row_max + jnp.log(row_sum))[..., 0])

    attended_heads, log_sums = lax.map(forward_block, (query_blocks, starts))
    attended = lax.all_to_all(
        attended_heads.reshape(group_rows, local_width),
        "seq",
        split_axis=0,
        concat_axis=1,
        tiled=True,
    )
    middle = inputs + jnp.dot(attended, out_weight, preferred_element_type=jnp.float32)
    time_embed = time_table(timestep.astype(jnp.float32), model_width).astype(jnp.bfloat16)
    modulation = jnp.dot(time_embed, ada_weight, preferred_element_type=jnp.float32)[0]
    mod_scale = modulation[:model_width]
    mod_shift = modulation[model_width : 2 * model_width]
    mod_gate = modulation[2 * model_width :]
    normed_two, scaling_two = layer_norm(middle)
    hidden_two = (normed_two * (1.0 + mod_scale) + mod_shift).astype(jnp.bfloat16)
    pre_act = jnp.dot(hidden_two, up_weight, preferred_element_type=jnp.float32)
    gelu_vals, gelu_pull = jax.vjp(lambda inner: jax.nn.gelu(inner, approximate=True), pre_act)
    activated = gelu_vals.astype(jnp.bfloat16)
    mlp_out = jnp.dot(activated, down_weight, preferred_element_type=jnp.float32)
    result = middle + mod_gate * mlp_out
    grad_out = out_grad.astype(jnp.float32)
    grad_mlp = (mod_gate * grad_out).astype(jnp.bfloat16)
    grad_gate = jnp.sum(grad_out * mlp_out, axis=0)
    grad_wdown = left_product(activated, grad_mlp)
    grad_act = right_product(grad_mlp, down_weight)
    grad_pre = gelu_pull(grad_act)[0].astype(jnp.bfloat16)
    grad_wup = left_product(hidden_two, grad_pre)
    grad_hidden_two = right_product(grad_pre, up_weight)
    grad_scale = jnp.sum(grad_hidden_two * normed_two, axis=0)
    grad_shift = jnp.sum(grad_hidden_two, axis=0)
    grad_middle = grad_out + norm_back(grad_hidden_two * (1.0 + mod_scale), normed_two, scaling_two)
    grad_mod = jnp.concatenate([grad_scale, grad_shift, grad_gate])
    grad_branch = grad_middle.astype(jnp.bfloat16)
    grad_wout = left_product(attended, grad_branch)
    grad_attn = right_product(grad_branch, out_weight).astype(jnp.bfloat16)
    grad_heads = lax.all_to_all(grad_attn, "seq", split_axis=1, concat_axis=0, tiled=True).reshape(
        blocks, block_rows, heads_local, HEAD_DIM
    )

    def backward_block(carry, operands):
        key_grad, value_grad = carry
        query_block, start, grad_block, lse_block = operands
        scores = scores_of(query_block, start)
        attn_probs = jnp.exp(scores - lse_block[..., None])
        value_grad = value_grad + jnp.einsum(
            "hqk,qhd->khd",
            attn_probs.astype(jnp.bfloat16),
            grad_block,
            preferred_element_type=jnp.float32,
        )
        prob_grad = jnp.einsum(
            "qhd,khd->hqk", grad_block, values_all, preferred_element_type=jnp.float32
        )
        row_centre = jnp.sum(attn_probs * prob_grad, axis=-1, keepdims=True)
        score_grad = (attn_probs * (prob_grad - row_centre)).astype(jnp.bfloat16)
        query_grad = (
            jnp.einsum("hqk,khd->qhd", score_grad, keys_all, preferred_element_type=jnp.float32)
            * 0.125
        )
        key_grad = (
            key_grad
            + jnp.einsum(
                "hqk,qhd->khd", score_grad, query_block, preferred_element_type=jnp.float32
            )
            * 0.125
        )
        return ((key_grad, value_grad), query_grad)

    zero_grad = jnp.zeros((group_rows, heads_local, HEAD_DIM), jnp.float32)
    (key_grad, value_grad), query_grads = lax.scan(
        backward_block, (zero_grad, zero_grad), (query_blocks, starts, grad_heads, log_sums)
    )
    stacked = jnp.stack(
        [query_grads.reshape(group_rows, heads_local, HEAD_DIM), key_grad, value_grad], axis=1
    )
    stacked = stacked.astype(jnp.bfloat16).reshape(group_rows, 3, 1, local_width)
    returned = (
        lax.all_to_all(stacked, "seq", split_axis=0, concat_axis=2, tiled=True)
        .astype(jnp.float32)
        .reshape(tok_rows, 3, HEADS, HEAD_DIM)
    )
    grad_qkv = jnp.stack(
        [
            rotate(returned[:, 0], cos_table, sine_table, -1.0),
            rotate(returned[:, 1], cos_table, sine_table, -1.0),
            returned[:, 2],
        ],
        axis=1,
    )
    grad_qkv = grad_qkv.reshape(tok_rows, 3 * model_width).astype(jnp.bfloat16)
    grad_wqkv = left_product(hidden_one, grad_qkv)
    grad_hidden_one = right_product(grad_qkv, qkv_weight)
    grad_gain = jnp.sum(grad_hidden_one * normed_one, axis=0)
    grad_inputs = grad_middle + norm_back(grad_hidden_one * gain_float, normed_one, scaling_one)
    qkv_cols = 3 * model_width
    grad_wada = time_embed.astype(jnp.float32).reshape(-1)[:, None] * grad_mod[None, :]
    grad_joint = jnp.concatenate([grad_wqkv, grad_wada], axis=1)
    data_count = lax.axis_size("dp")
    parts = (
        lax.psum_scatter(
            split_rows(grad_gain, data_count).astype(jnp.bfloat16),
            "seq",
            scatter_dimension=1,
            tiled=True,
        ).astype(jnp.float32),
        lax.psum_scatter(
            split_rows(grad_joint, data_count).astype(jnp.bfloat16),
            "seq",
            scatter_dimension=1,
            tiled=True,
        ).astype(jnp.float32),
        lax.psum_scatter(
            split_rows(grad_wout, data_count).astype(jnp.bfloat16),
            "seq",
            scatter_dimension=1,
            tiled=True,
        ).astype(jnp.float32),
        lax.psum_scatter(
            split_rows(grad_wup, data_count).astype(jnp.bfloat16),
            "seq",
            scatter_dimension=1,
            tiled=True,
        ).astype(jnp.float32),
        lax.psum_scatter(
            split_rows(grad_wdown, data_count).astype(jnp.bfloat16),
            "seq",
            scatter_dimension=1,
            tiled=True,
        ).astype(jnp.float32),
    )
    owned = (
        lax.psum_scatter(parts[0], "dp", scatter_dimension=0, tiled=True),
        lax.psum_scatter(parts[1], "dp", scatter_dimension=0, tiled=True),
        lax.psum_scatter(parts[2], "dp", scatter_dimension=0, tiled=True),
        lax.psum_scatter(parts[3], "dp", scatter_dimension=0, tiled=True),
        lax.psum_scatter(parts[4], "dp", scatter_dimension=0, tiled=True),
    )
    spread = (
        lax.all_gather(owned[0].astype(jnp.bfloat16), "seq", axis=1, tiled=True).astype(
            jnp.float32
        ),
        lax.all_gather(owned[1].astype(jnp.bfloat16), "seq", axis=1, tiled=True).astype(
            jnp.float32
        ),
        lax.all_gather(owned[2].astype(jnp.bfloat16), "seq", axis=1, tiled=True).astype(
            jnp.float32
        ),
        lax.all_gather(owned[3].astype(jnp.bfloat16), "seq", axis=1, tiled=True).astype(
            jnp.float32
        ),
        lax.all_gather(owned[4].astype(jnp.bfloat16), "seq", axis=1, tiled=True).astype(
            jnp.float32
        ),
    )
    final_gain = spread[0].reshape(-1)
    final_joint = spread[1].reshape(spread[1].shape[1], -1)
    final_out = spread[2].reshape(spread[2].shape[1], -1)
    final_up = spread[3].reshape(spread[3].shape[1], -1)
    final_down = spread[4].reshape(spread[4].shape[1], -1)
    final_qkv = final_joint[:, :qkv_cols]
    final_ada = final_joint[:, qkv_cols:]
    return (
        result.astype(jnp.bfloat16),
        grad_inputs.astype(jnp.bfloat16),
        final_gain,
        final_qkv,
        final_out,
        final_ada,
        final_up,
        final_down,
    )


def solution(mesh):
    placed = (
        P(("dp", "seq"), None),
        P("dp"),
        P("dp", None),
        P("dp", None),
        P("dp", None),
        P("dp", None),
        P("dp", None),
        P(("dp", "seq"), None),
        P("dp", None),
        P("dp"),
    )
    return jax.shard_map(
        body,
        mesh=mesh,
        in_specs=placed,
        out_specs=(
            P(("dp", "seq"), None),
            P(("dp", "seq"), None),
            P("dp"),
            P("dp", None),
            P("dp", None),
            P("dp", None),
            P("dp", None),
            P("dp", None),
        ),
        check_vma=False,
    )
```

profile of v0, /device:TPU:0, one launch (start us, length us, event | category | flops | bytes accessed | tf_op | source)
XLA Modules:
  0.0 863.8 jit_solution(9710499089409813553)
XLA Ops:
  12.9 23.2 %all-reduce = bf16[768]{0:T(1024)(128)(2,1)S(1)} all-reduce(bf16[768]{0:T(1024)(128)(2,1)S(1)} %dynamic-update-slice), channel_id=1, replica_groups=mesh['dp'=8,'seq'=4] {'dp'}, use_global_device_ids=true, to_apply=%add | all-reduce | flops 768 | bytes 3072
  39.3 39.0 %all-gather.6.cloned.1.call-done = bf16[768,2304]{1,0:T(8,128)(2,1)} async-done(((bf16[96,2304]{1,0:T(8,128)(2,1)}), bf16[768,2304]{1,0:T(8,128)(2,1)}) %all-gather.6.cloned.1.call-update) | async-done | bytes 3538960 | tf_op jit(solution)/shard_map/all_gather | solution.py:96
  89.9 13.3 %all-to-all-done = bf16[256,3,4,192]{0,3,1,2:T(8,128)(2,1)S(1)} async-done(((bf16[256,3,4,192]{0,3,1,2:T(8,128)(2,1)}), bf16[256,3,4,192]{0,3,1,2:T(8,128)(2,1)S(1)}, u32[]{:S(2)}, u32[]{:S(2)}) %all-to-all-start) | async-done | bytes 1179680 | tf_op jit(solution)/shard_map/all_to_all | solution.py:122
  106.9 25.5 %while.30 = (s32[]{:T(128)}, bf16[2,512,3,64]{1,3,2,0:T(8,128)(2,1)S(1)}, f32[2,3,512]{2,1,0:T(4,128)}, s32[]{:T(128)}, s32[2]{0:T(128)S(1)}, /*index=5*/s32[]{:...) while((s32[]{:T(128)}, ...), condition=%wide.region_5.6_spmd.clone.clone, body=%wide.region_2.5_spmd.clone.clone.sunk | while | flops 422682112 | bytes 22220956 | solution.py:156
  137.8 6.4 all-gather.10.cloned.1.call-done
  146.8 39.1 %all-gather.8.cloned.1.call-done = bf16[768,768]{1,0:T(8,128)(2,1)} async-done(((bf16[96,768]{1,0:T(8,128)(2,1)}), bf16[768,768]{1,0:T(8,128)(2,1)}) %all-gather.8.cloned.1.call-update) | async-done | bytes 1179664 | tf_op jit(solution)/shard_map/all_gather | solution.py:97
  188.1 78.6 %all-gather.12.cloned.1.call-done = bf16[768,3072]{1,0:T(8,128)(2,1)} async-done(((bf16[96,3072]{1,0:T(8,128)(2,1)}), bf16[768,3072]{1,0:T(8,128)(2,1)}) %all-gather.12.cloned.1.call-update) | async-done | bytes 4718608 | tf_op jit(solution)/shard_map/all_gather | solution.py:101
  272.2 74.6 %all-gather.14.cloned.1.call-done = bf16[3072,768]{1,0:T(8,128)(2,1)} async-done(((bf16[384,768]{1,0:T(8,128)(2,1)}), bf16[3072,768]{1,0:T(8,128)(2,1)}) %all-gather.14.cloned.1.call-update) | async-done | bytes 4718608 | tf_op jit(solution)/shard_map/all_gather | solution.py:102
  346.8 6.7 fusion.56
  362.6 6.4 convolution_convert_fusion
  387.8 45.0 %while.31 = (s32[]{:T(128)}, f32[1024,3,64]{0,2,1:T(8,128)}, f32[1024,3,64]{0,2,1:T(8,128)}, bf16[2,512,3,64]{1,3,2,0:T(8,128)(2,1)}, bf16[2,512,3,64]{1,3,2,0:T...) while((s32[]{:T(128)}, f32[1024,3,64]{0,2,1:T(8,128)}, ...), condition=%wide.region_12.13_spmd.clone.clone, body=%wide.region_10.12_spmd.clone.clone.sunk | while | flops 1032363520 | bytes 110420320 | solution.py:226
  445.6 30.9 %all-to-all-done.3 = bf16[1024,3,1,192]{3,1,2,0:T(4,128)(2,1)S(1)} async-done(((bf16[1024,3,1,192]{3,1,2,0:T(4,128)(2,1)}), bf16[1024,3,1,192]{3,1,2,0:T(4,128)(2,1)S(1)}, u32[]{:S(2)}, u32[]{:S(2)}) %all-to-all-start.3) | async-done | bytes 1179680 | tf_op jit(solution)/shard_map/all_to_all | solution.py:234
  488.0 6.7 copy.95
  501.7 56.8 %reduce-scatter.27.cloned.1.call-done = bf16[24,36864]{1,0:T(8,128)(2,1)} async-done(((bf16[96,36864]{1,0:T(8,128)(2,1)}), bf16[24,36864]{1,0:T(8,128)(2,1)}) %reduce-scatter.27.cloned.1.call-update) | async-done | bytes 1769488
  567.8 5.7 all-reduce.2
  573.6 21.7 %all-reduce.3 = bf16[8,24,1]{1,0,2:T(8,128)(2,1)S(1)} all-reduce(f32[8,24,1]{1,0,2:T(8,128)S(1)} %dynamic-slice_convert_fusion), channel_id=3, replica_groups=mesh['dp'=8,'seq'=4] {'dp'}, use_global_device_ids=true, to_apply=%region_17.18.clone | all-reduce | flops 192 | bytes 1152
  596.2 5.6 all-reduce.1
  603.4 21.1 %reduce-scatter.19.cloned.1.call-done = f32[1,24,768]{2,1,0:T(8,128)} async-done(((f32[8,24,768]{2,1,0:T(8,128)}), f32[1,24,768]{2,1,0:T(8,128)}) %reduce-scatter.19.cloned.1.call-update) | async-done | bytes 73744 | tf_op jit(solution)/shard_map/reduce_scatter | solution.py:290
  631.5 59.9 %reduce-scatter.25.cloned.1.call-done = bf16[1,96,768]{2,1,0:T(8,128)(2,1)} async-done(((bf16[8,96,768]{2,1,0:T(8,128)(2,1)}), bf16[1,96,768]{2,1,0:T(8,128)(2,1)}) %reduce-scatter.25.cloned.1.call-update) | async-done | bytes 147472 | tf_op jit(solution)/shard_map/reduce_scatter | solution.py:292
  691.4 7.7 all_gather.43
  700.2 63.0 %reduce-scatter.21.cloned.1.call-done = f32[1,24,3072]{2,1,0:T(8,128)} async-done(((f32[8,24,3072]{2,1,0:T(8,128)}), f32[1,24,3072]{2,1,0:T(8,128)}) %reduce-scatter.21.cloned.1.call-update) | async-done | bytes 294928 | tf_op jit(solution)/shard_map/reduce_scatter | solution.py:291
  764.2 7.5 all_gather.42
  772.8 72.6 %reduce-scatter.17.cloned.1.call-done = f32[1,24,4608]{2,1,0:T(8,128)} async-done(((f32[8,24,4608]{2,1,0:T(8,128)}), f32[1,24,4608]{2,1,0:T(8,128)}) %reduce-scatter.17.cloned.1.call-update) | async-done | bytes 442384 | tf_op jit(solution)/shard_map/reduce_scatter | solution.py:289
  846.5 9.1 %all_gather.40 = bf16[1,96,4608]{2,1,0:T(8,128)(2,1)S(1)} all-gather(bf16[1,24,4608]{2,1,0:T(8,128)(2,1)S(1)} %convert_element_type.256), channel_id=1, replica_groups=mesh['dp'=8,'seq'=4] {'seq'}, dimensions={1}, use_global_device_ids=true | all-gather | bytes 1105920 | tf_op jit(solution)/shard_map/all_gather | solution.py:298
  (250 shorter events, 190.5 us)
Async XLA Ops:
  7.2 71.1 %all-gather.6.cloned.1.call-start = ((), (), s32[]{:S(2)}) async-start(), calls=%async_computation.12 | async-start | bytes 3981312 | tf_op jit(solution)/shard_map/all_gather | solution.py:96
  7.9 136.3 %all-gather.10.cloned.1.call-start = ((), (), s32[]{:S(2)}) async-start(), calls=%async_computation.14 | async-start | bytes 3981312 | tf_op jit(solution)/shard_map/all_gather | solution.py:100
  8.6 177.3 %all-gather.8.cloned.1.call-start = ((), (), s32[]{:S(2)}) async-start(), calls=%async_computation.13 | async-start | bytes 1327104 | tf_op jit(solution)/shard_map/all_gather | solution.py:97
  9.4 257.3 %all-gather.12.cloned.1.call-start = ((), (), s32[]{:S(2)}) async-start(), calls=%async_computation.15 | async-start | bytes 5308416 | tf_op jit(solution)/shard_map/all_gather | solution.py:101
  36.1 46.0 %copy-start.13 = (f32[768]{0:T(1024)}, f32[768]{0:T(1024)S(1)}, u32[]{:S(2)}) copy-start(f32[768]{0:T(1024)S(1)} %convert_element_type.231) | copy-start | bytes 9220
  37.2 44.8 %copy-start.16 = (f32[256]{0:T(256)}, f32[256]{0:T(256)S(1)}, u32[]{:S(2)}) copy-start(f32[256]{0:T(256)S(1)} %broadcast_multiply_fusion.6) | copy-start | bytes 3076
  38.5 43.6 %copy-start.18 = (f32[256]{0:T(256)}, f32[256]{0:T(256)S(1)}, u32[]{:S(2)}) copy-start(f32[256]{0:T(256)S(1)} %add_rsqrt_fusion.1) | copy-start | bytes 3076
  39.3 42.9 %copy-start.11 = (f32[256,32]{0,1:T(8,128)}, f32[256,32]{0,1:T(8,128)S(1)}, u32[]{:S(2)}) copy-start(f32[256,32]{0,1:T(8,128)S(1)} %get-tuple-element.453) | copy-start | bytes 98308
  83.8 19.4 %all-to-all-start = ((bf16[256,3,4,192]{0,3,1,2:T(8,128)(2,1)}), bf16[256,3,4,192]{0,3,1,2:T(8,128)(2,1)S(1)}, u32[]{:S(2)}, u32[]{:S(2)}) async-start(bf16[256,3,4,192]{0,3,1,2:T(8,128)(2,1)} %copy.70), calls=%async_computation | async-start | bytes 2359296 | tf_op jit(solution)/shard_map/all_to_all | solution.py:122
  87.4 259.4 %all-gather.14.cloned.1.call-start = ((), (), s32[]{:S(2)}) async-start(), calls=%async_computation.16 | async-start | bytes 5308416 | tf_op jit(solution)/shard_map/all_gather | solution.py:102
  132.8 53.2 %copy-start.3 = (bf16[256,768]{1,0:T(8,128)(2,1)S(1)}, bf16[256,768]{1,0:T(8,128)(2,1)}, u32[]{:S(2)}) copy-start(bf16[256,768]{1,0:T(8,128)(2,1)} %param.14) | copy-start | bytes 1179652
  133.8 52.2 %all-to-all-start.1 = ((bf16[4,256,192]{1,2,0:T(8,128)(2,1)}), bf16[4,256,192]{1,2,0:T(8,128)(2,1)S(1)}, u32[]{:S(2)}, u32[]{:S(2)}) async-start(bf16[4,256,192]{1,2,0:T(8,128)(2,1)} %copy.74), calls=%async_computation.1 | async-start | bytes 786432 | tf_op jit(solution)/shard_map/all_to_all | solution.py:157
  137.2 357.6 %reduce-scatter.29.cloned.1.call-start = ((), (), s32[]{:S(2)}) async-start(), calls=%async_computation.23 | async-start | bytes 1474560
  266.7 80.1 %copy-start.27 = (bf16[256,768]{1,0:T(8,128)(2,1)S(1)}, bf16[256,768]{1,0:T(8,128)(2,1)}, u32[]{:S(2)}) copy-start(bf16[256,768]{1,0:T(8,128)(2,1)} %param.21) | copy-start | bytes 1179652
  362.5 134.3 %reduce-scatter.23.cloned.1.call-start = ((), (), s32[]{:S(2)}) async-start(), calls=%async_computation.20 | async-start | bytes 5898240 | tf_op jit(solution)/shard_map/reduce_scatter | solution.py:280
  371.7 14.7 %all-to-all-start.2 = ((bf16[256,4,192]{0,2,1:T(8,128)(2,1)}), bf16[256,4,192]{0,2,1:T(8,128)(2,1)S(1)}, u32[]{:S(2)}, u32[]{:S(2)}) async-start(bf16[256,4,192]{0,2,1:T(8,128)(2,1)} %bitcast.16), calls=%async_computation.2 | async-start | bytes 786432 | tf_op jit(solution)/shard_map/all_to_all | solution.py:192
  375.1 122.4 %reduce-scatter.31.cloned.1.call-start = ((), (), s32[]{:S(2)}) async-start(), calls=%async_computation.24 | async-start | bytes 5898240
  439.5 37.0 %all-to-all-start.3 = ((bf16[1024,3,1,192]{3,1,2,0:T(4,128)(2,1)}), bf16[1024,3,1,192]{3,1,2,0:T(4,128)(2,1)S(1)}, u32[]{:S(2)}, u32[]{:S(2)}) async-start(bf16[1024,3,1,192]{3,1,2,0:T(4,128)(2,1)} %copy.80), calls=%async_computation.3 | async-start | bytes 4194304 | tf_op jit(solution)/shard_map/all_to_all | solution.py:234
  443.1 115.4 %reduce-scatter.27.cloned.1.call-start = ((), (), s32[]{:S(2)}) async-start(), calls=%async_computation.22 | async-start | bytes 8847360
  494.8 129.7 %reduce-scatter.19.cloned.1.call-start = ((), (), s32[]{:S(2)}) async-start(), calls=%async_computation.18 | async-start | bytes 663552 | tf_op jit(solution)/shard_map/reduce_scatter | solution.py:290
  496.8 194.6 %reduce-scatter.25.cloned.1.call-start = ((), (), s32[]{:S(2)}) async-start(), calls=%async_computation.21 | async-start | bytes 1327104 | tf_op jit(solution)/shard_map/reduce_scatter | solution.py:292
  497.5 265.7 %reduce-scatter.21.cloned.1.call-start = ((), (), s32[]{:S(2)}) async-start(), calls=%async_computation.19 | async-start | bytes 2654208 | tf_op jit(solution)/shard_map/reduce_scatter | solution.py:291
  501.7 343.8 %reduce-scatter.17.cloned.1.call-start = ((), (), s32[]{:S(2)}) async-start(), calls=%async_computation.17 | async-start | bytes 3981312 | tf_op jit(solution)/shard_map/reduce_scatter | solution.py:289
  564.2 38.1 %copy-start.6 = (f32[256,768]{1,0:T(8,128)S(1)}, f32[256,768]{1,0:T(8,128)}, u32[]{:S(2)}) copy-start(f32[256,768]{1,0:T(8,128)} %copy-done.5) | copy-start | bytes 2359300
  (29 other events, 127.0 us)
Sparse Core Ops, SparseCore 0:
  10.2 68.0 all-gather.5
  80.5 63.6 all-gather.9
  146.4 39.5 all-gather.7
  188.0 78.6 all-gather.11
  268.7 78.0 all-gather.13
  362.6 27.1 reduce-scatter.28
  392.6 45.1 reduce-scatter.22
  440.3 55.2 reduce-scatter.30
  498.2 60.2 reduce-scatter.26
  562.2 62.1 reduce-scatter.18
  628.2 63.1 reduce-scatter.24
  695.2 67.9 reduce-scatter.20
  767.3 78.1 reduce-scatter.16
where the time goes:
time: 873 us; the launch traced here: 864 us
  waiting for transfers between devices  565 us (65%)
  blocking collectives  86 us (10%)
  matrix products  79.7 us (9%)
  other arithmetic  53.6 us (6%)
  local copies, waits for them, and re-layouts  46.8 us (5%)
  between operations  17.3 us (2%)
  starting transfers between devices  15.4 us (2%)
    all_gather x1, waiting for transfers between devices, body(): lax.all_gather(w_up, 'dp', axis=0, tiled=True)  78.6 us
    all_gather x1, waiting for transfers between devices, body(): lax.all_gather(w_down, 'dp', axis=0, tiled=True)  74.6 us
    reduce_scatter x1, waiting for transfers between devices, body(): lax.psum_scatter(parts[1], 'dp', scatter_dimension=0, tiled=True)  72.6 us
    reduce_scatter x1, waiting for transfers between devices, body(): lax.psum_scatter(parts[3], 'dp', scatter_dimension=0, tiled=True)  63 us
    unnamed x16, waiting for transfers between devices  60.7 us
    reduce_scatter x1, waiting for transfers between devices, body(): lax.psum_scatter(parts[4], 'dp', scatter_dimension=0, tiled=True)  59.9 us
    unnamed x4, blocking collectives  56.3 us
    all_gather x1, waiting for transfers between devices, body(): lax.all_gather(w_out, 'dp', axis=0, tiled=True)  39.1 us
  transfers between devices with their start and end apart: 17, of which 13 were waited for; matrix products, arithmetic and copies ran while one was open for 18% of the time, Pallas kernels for 0%

commit v1 on v0

--- a/solution.py
+++ b/solution.py
@@ -96,10 +96,23 @@
         lax.all_gather(w_qkv, "dp", axis=0, tiled=True),
         lax.all_gather(w_out, "dp", axis=0, tiled=True),
     )
+
+    def _read_clusters(packet, axis_name):
+        n_all = lax.axis_size(axis_name)
+        gallery = [(idx, (idx + 1) % n_all) for idx in range(n_all)]
+        nodes = [(idx, (idx - 1) % n_all) for idx in range(n_all)]
+        row_out, state_now = ([packet], [packet])
+        for _ in range(n_all // 2):
+            row_out.append(lax.ppermute(row_out[-1], axis_name, gallery))
+        for _ in range((n_all - 1) // 2):
+            state_now.append(lax.ppermute(state_now[-1], axis_name, nodes))
+        known = jnp.concatenate([*row_out[::-1], *state_now[1:]], axis=0)
+        return jnp.roll(known, (lax.axis_index(axis_name) - n_all // 2) * packet.shape[0], axis=0)
+
     ada_weight, up_weight, down_weight = (
         lax.all_gather(w_ada, "dp", axis=0, tiled=True),
         lax.all_gather(w_up, "dp", axis=0, tiled=True),
-        lax.all_gather(w_down, "dp", axis=0, tiled=True),
+        _read_clusters(w_down, "dp"),
     )
     gain_float = gain_full.astype(jnp.float32)
     inputs = tokens.astype(jnp.float32)

time: 873 us -> 846 us (0.969)
  waiting for transfers between devices: 565 us -> 489 us
  local copies, waits for them, and re-layouts: 46.8 us -> 63.6 us
  blocking collectives: 86 us -> 101 us
  starting transfers between devices: 15.4 us -> 28.7 us
    all_gather x1 -> x0, waiting for transfers between devices: 74.6 us -> none  [body(): lax.all_gather(w_down, 'dp', axis=0, tiled=True)]
    ppermute x0 -> x7, waiting for transfers between devices: none -> 60.8 us  [the longest x4 42 us: _read_clusters(): row_out.append(lax.ppermute(row_out[-1], axis_name, gallery))]
    all_gather x1, waiting for transfers between devices: 39 us -> 0.01 us  [body(): lax.all_gather(w_qkv, 'dp', axis=0, tiled=True)]
    unnamed x66 -> x99, local copies, waits for them, and re-layouts: 24 us -> 39 us
    unnamed x4, blocking collectives: 56.3 us -> 70.9 us
    ppermute x0 -> x7, starting transfers between devices: none -> 13.5 us  [the longest x4 7.76 us: _read_clusters(): row_out.append(lax.ppermute(row_out[-1], axis_name, gallery))]
    all_gather x1, waiting for transfers between devices: 39.1 us -> 29.8 us  [body(): lax.all_gather(w_out, 'dp', axis=0, tiled=True)]
    unnamed x16 -> x15, waiting for transfers between devices: 60.7 us -> 59.1 us
  transfers between devices with their start and end apart: 17 -> 23, of which waited for: 13 -> 15; matrix products, arithmetic and copies ran while one was open for 18% -> 20% of each run, Pallas kernels for 0% -> 0%
where the time goes in v1:
time: 846 us; the launch traced here: 836 us
  waiting for transfers between devices  489 us (58%)
  blocking collectives  101 us (12%)
  matrix products  81.4 us (10%)
  local copies, waits for them, and re-layouts  63.6 us (8%)
  other arithmetic  54.3 us (6%)
  starting transfers between devices  28.7 us (3%)
  between operations  18 us (2%)
    all_gather x1, waiting for transfers between devices, body(): lax.all_gather(w_up, 'dp', axis=0, tiled=True)  78.6 us
    reduce_scatter x1, waiting for transfers between devices, body(): lax.psum_scatter(parts[1], 'dp', scatter_dimension=0, tiled=True)  72.6 us
    unnamed x4, blocking collectives  70.9 us
    reduce_scatter x1, waiting for transfers between devices, body(): lax.psum_scatter(parts[3], 'dp', scatter_dimension=0, tiled=True)  63.3 us
    reduce_scatter x1, waiting for transfers between devices, body(): lax.psum_scatter(parts[4], 'dp', scatter_dimension=0, tiled=True)  59.7 us
    unnamed x15, waiting for transfers between devices  59.1 us
    ppermute x4, waiting for transfers between devices, _read_clusters(): row_out.append(lax.ppermute(row_out[-1], axis_name, gallery))  42 us
    unnamed x99, local copies, waits for them, and re-layouts  39 us
  transfers between devices with their start and end apart: 23, of which 15 were waited for; matrix products, arithmetic and copies ran while one was open for 20% of the time, Pallas kernels for 0%

profile of v1, /device:TPU:0, one launch (start us, length us, event | category | flops | bytes accessed | tf_op | source)
XLA Modules:
  0.0 835.7 jit_solution(13166399848430753878)
XLA Ops:
  12.5 19.8 %collective-permute-done = bf16[384,768]{1,0:T(8,128)(2,1)S(1)} collective-permute-done((bf16[384,768]{1,0:T(8,128)(2,1)}, bf16[384,768]{1,0:T(8,128)(2,1)S(1)}, u32[]{:S(2)}, u32[]{:S(2)}) %collective-permute-start) | collective-permute-done | bytes 589856 | tf_op jit(solution)/shard_map/ppermute | solution.py:106
  38.9 21.7 %collective-permute-done.1 = bf16[384,768]{1,0:T(8,128)(2,1)S(1)} collective-permute-done((bf16[384,768]{1,0:T(8,128)(2,1)S(1)}, bf16[384,768]{1,0:T(8,128)(2,1)S(1)}, u32[]{:S(2)}, u32[]{:S(2)}) %collective-permute-start.1) | collective-permute-done | bytes 589856 | tf_op jit(solution)/shard_map/ppermute | solution.py:106
  66.0 37.7 %all-reduce = bf16[768]{0:T(1024)(128)(2,1)S(1)} all-reduce(bf16[768]{0:T(1024)(128)(2,1)S(1)} %dynamic-update-slice), channel_id=1, replica_groups=mesh['dp'=8,'seq'=4] {'dp'}, use_global_device_ids=true, to_apply=%add | all-reduce | flops 768 | bytes 3072
  110.5 15.6 %collective-permute-done.5 = bf16[384,768]{1,0:T(8,128)(2,1)S(1)} collective-permute-done((bf16[384,768]{1,0:T(8,128)(2,1)S(1)}, bf16[384,768]{1,0:T(8,128)(2,1)S(1)}, u32[]{:S(2)}, u32[]{:S(2)}) %collective-permute-start.5) | collective-permute-done | bytes 589856 | tf_op jit(solution)/shard_map/ppermute | solution.py:108
  157.5 7.5 all-to-all-done
  168.7 25.4 %while.30 = (s32[]{:T(128)}, bf16[2,512,3,64]{1,3,2,0:T(8,128)(2,1)S(1)}, f32[2,3,512]{2,1,0:T(4,128)}, s32[]{:T(128)}, s32[2]{0:T(128)S(1)}, /*index=5*/s32[]{:...) while((s32[]{:T(128)}, ...), condition=%wide.region_5.6_spmd.clone.clone, body=%wide.region_2.5_spmd.clone.clone.sunk | while | flops 422682112 | bytes 22220956 | solution.py:169
  201.7 29.8 %all-gather.7.cloned.1.call-done = bf16[768,768]{1,0:T(8,128)(2,1)} async-done(((bf16[96,768]{1,0:T(8,128)(2,1)}), bf16[768,768]{1,0:T(8,128)(2,1)}) %all-gather.7.cloned.1.call-update) | async-done | bytes 1179664 | tf_op jit(solution)/shard_map/all_gather | solution.py:97
  233.6 78.6 %all-gather.11.cloned.1.call-done = bf16[768,3072]{1,0:T(8,128)(2,1)} async-done(((bf16[96,3072]{1,0:T(8,128)(2,1)}), bf16[768,3072]{1,0:T(8,128)(2,1)}) %all-gather.11.cloned.1.call-update) | async-done | bytes 4718608 | tf_op jit(solution)/shard_map/all_gather | solution.py:114
  316.2 7.2 fusion.60
  325.7 6.3 fusion.78
  333.6 6.4 convolution_convert_fusion
  359.0 45.2 %while.31 = (s32[]{:T(128)}, f32[1024,3,64]{0,2,1:T(8,128)}, f32[1024,3,64]{0,2,1:T(8,128)}, bf16[2,512,3,64]{1,3,2,0:T(8,128)(2,1)}, bf16[2,512,3,64]{1,3,2,0:T...) while((s32[]{:T(128)}, f32[1024,3,64]{0,2,1:T(8,128)}, ...), condition=%wide.region_12.13_spmd.clone.clone, body=%wide.region_10.12_spmd.clone.clone.sunk | while | flops 1032363520 | bytes 110420320 | solution.py:239
  417.3 31.1 %all-to-all-done.3 = bf16[1024,3,1,192]{3,1,2,0:T(4,128)(2,1)S(1)} async-done(((bf16[1024,3,1,192]{3,1,2,0:T(4,128)(2,1)}), bf16[1024,3,1,192]{3,1,2,0:T(4,128)(2,1)S(1)}, u32[]{:S(2)}, u32[]{:S(2)}) %all-to-all-start.3) | async-done | bytes 1179680 | tf_op jit(solution)/shard_map/all_to_all | solution.py:247
  459.9 6.7 copy.95
  473.5 56.3 %reduce-scatter.27.cloned.1.call-done = bf16[24,36864]{1,0:T(8,128)(2,1)} async-done(((bf16[96,36864]{1,0:T(8,128)(2,1)}), bf16[24,36864]{1,0:T(8,128)(2,1)}) %reduce-scatter.27.cloned.1.call-update) | async-done | bytes 1769488
  539.1 5.7 all-reduce.2
  544.9 21.8 %all-reduce.3 = bf16[8,24,1]{1,0,2:T(8,128)(2,1)S(1)} all-reduce(f32[8,24,1]{1,0,2:T(8,128)S(1)} %dynamic-slice_convert_fusion), channel_id=3, replica_groups=mesh['dp'=8,'seq'=4] {'dp'}, use_global_device_ids=true, to_apply=%region_17.18.clone | all-reduce | flops 192 | bytes 1152
  574.9 21.0 %reduce-scatter.19.cloned.1.call-done = f32[1,24,768]{2,1,0:T(8,128)} async-done(((f32[8,24,768]{2,1,0:T(8,128)}), f32[1,24,768]{2,1,0:T(8,128)}) %reduce-scatter.19.cloned.1.call-update) | async-done | bytes 73744 | tf_op jit(solution)/shard_map/reduce_scatter | solution.py:303
  602.9 59.7 %reduce-scatter.25.cloned.1.call-done = bf16[1,96,768]{2,1,0:T(8,128)(2,1)} async-done(((bf16[8,96,768]{2,1,0:T(8,128)(2,1)}), bf16[1,96,768]{2,1,0:T(8,128)(2,1)}) %reduce-scatter.25.cloned.1.call-update) | async-done | bytes 147472 | tf_op jit(solution)/shard_map/reduce_scatter | solution.py:305
  662.6 7.7 all_gather.39
  671.4 63.3 %reduce-scatter.21.cloned.1.call-done = f32[1,24,3072]{2,1,0:T(8,128)} async-done(((f32[8,24,3072]{2,1,0:T(8,128)}), f32[1,24,3072]{2,1,0:T(8,128)}) %reduce-scatter.21.cloned.1.call-update) | async-done | bytes 294928 | tf_op jit(solution)/shard_map/reduce_scatter | solution.py:304
  735.7 7.5 all_gather.38
  744.2 72.6 %reduce-scatter.17.cloned.1.call-done = f32[1,24,4608]{2,1,0:T(8,128)} async-done(((f32[8,24,4608]{2,1,0:T(8,128)}), f32[1,24,4608]{2,1,0:T(8,128)}) %reduce-scatter.17.cloned.1.call-update) | async-done | bytes 442384 | tf_op jit(solution)/shard_map/reduce_scatter | solution.py:302
  817.9 9.1 %all_gather.36 = bf16[1,96,4608]{2,1,0:T(8,128)(2,1)S(1)} all-gather(bf16[1,24,4608]{2,1,0:T(8,128)(2,1)S(1)} %convert_element_type.256), channel_id=1, replica_groups=mesh['dp'=8,'seq'=4] {'seq'}, dimensions={1}, use_global_device_ids=true | all-gather | bytes 1105920 | tf_op jit(solution)/shard_map/all_gather | solution.py:311
  (296 shorter events, 224.4 us)
Async XLA Ops:
  7.2 132.4 %all-gather.5.cloned.1.call-start = ((), (), s32[]{:S(2)}) async-start(), calls=%async_computation.12 | async-start | bytes 3981312 | tf_op jit(solution)/shard_map/all_gather | solution.py:96
  7.9 191.2 %all-gather.9.cloned.1.call-start = ((), (), s32[]{:S(2)}) async-start(), calls=%async_computation.14 | async-start | bytes 3981312 | tf_op jit(solution)/shard_map/all_gather | solution.py:113
  8.7 222.9 %all-gather.7.cloned.1.call-start = ((), (), s32[]{:S(2)}) async-start(), calls=%async_computation.13 | async-start | bytes 1327104 | tf_op jit(solution)/shard_map/all_gather | solution.py:97
  9.4 121.8 %copy-start.8 = (bf16[384,768]{1,0:T(8,128)(2,1)S(1)}, bf16[384,768]{1,0:T(8,128)(2,1)}, u32[]{:S(2)}) copy-start(bf16[384,768]{1,0:T(8,128)(2,1)} %param.20) | copy-start | bytes 1769476
  9.4 302.9 %all-gather.11.cloned.1.call-start = ((), (), s32[]{:S(2)}) async-start(), calls=%async_computation.15 | async-start | bytes 5308416 | tf_op jit(solution)/shard_map/all_gather | solution.py:114
  9.4 22.8 %collective-permute-start = (bf16[384,768]{1,0:T(8,128)(2,1)}, bf16[384,768]{1,0:T(8,128)(2,1)S(1)}, u32[]{:S(2)}, u32[]{:S(2)}) collective-permute-start(bf16[384,768]{1,0:T(8,128)(2,1)} %param.20), channel_id=1, source_target_pairs={{0,4},{4,8},{8,12},{12,16},{16,20},{20,24},{24,28},{28,0},{1,5},{5... | collective-permute-start | bytes 1769480 | tf_op jit(solution)/shard_map/ppermute | solution.py:106
  32.2 28.4 %collective-permute-start.1 = (bf16[384,768]{1,0:T(8,128)(2,1)S(1)}, bf16[384,768]{1,0:T(8,128)(2,1)S(1)}, u32[]{:S(2)}, u32[]{:S(2)}) collective-permute-start(bf16[384,768]{1,0:T(8,128)(2,1)S(1)} %collective-permute-done), channel_id=1, source_target_pairs={{0,4},{4,8},{8,12},{12,16},{16,20},{20,24},{24,28},{28,0},{1,5},{5... | collective-permute-start | bytes 1769480 | tf_op jit(solution)/shard_map/ppermute | solution.py:106
  32.5 73.8 %collective-permute-start.4 = (bf16[384,768]{1,0:T(8,128)(2,1)}, bf16[384,768]{1,0:T(8,128)(2,1)S(1)}, u32[]{:S(2)}, u32[]{:S(2)}) collective-permute-start(bf16[384,768]{1,0:T(8,128)(2,1)} %param.20), channel_id=1, source_target_pairs={{0,28},{4,0},{8,4},{12,8},{16,12},{20,16},{24,20},{28,24},{1,29},{... | collective-permute-start | bytes 1769480 | tf_op jit(solution)/shard_map/ppermute | solution.py:108
  60.6 45.8 %collective-permute-start.2 = (bf16[384,768]{1,0:T(8,128)(2,1)S(1)}, bf16[384,768]{1,0:T(8,128)(2,1)S(1)}, u32[]{:S(2)}, u32[]{:S(2)}) collective-permute-start(bf16[384,768]{1,0:T(8,128)(2,1)S(1)} %collective-permute-done.1), channel_id=1, source_target_pairs={{0,4},{4,8},{8,12},{12,16},{16,20},{20,24},{24,28},{28,0},{1,5},{5... | collective-permute-start | bytes 1769480 | tf_op jit(solution)/shard_map/ppermute | solution.py:106
  106.3 19.8 %collective-permute-start.5 = (bf16[384,768]{1,0:T(8,128)(2,1)S(1)}, bf16[384,768]{1,0:T(8,128)(2,1)S(1)}, u32[]{:S(2)}, u32[]{:S(2)}) collective-permute-start(bf16[384,768]{1,0:T(8,128)(2,1)S(1)} %collective-permute-done.4), channel_id=1, source_target_pairs={{0,28},{4,0},{8,4},{12,8},{16,12},{20,16},{24,20},{28,24},{1,29},{... | collective-permute-start | bytes 1769480 | tf_op jit(solution)/shard_map/ppermute | solution.py:108
  106.4 21.4 %collective-permute-start.3 = (bf16[384,768]{1,0:T(8,128)(2,1)S(1)}, bf16[384,768]{1,0:T(8,128)(2,1)S(1)}, u32[]{:S(2)}, u32[]{:S(2)}) collective-permute-start(bf16[384,768]{1,0:T(8,128)(2,1)S(1)} %collective-permute-done.2), channel_id=1, source_target_pairs={{0,4},{4,8},{8,12},{12,16},{16,20},{20,24},{24,28},{28,0},{1,5},{5... | collective-permute-start | bytes 1769480 | tf_op jit(solution)/shard_map/ppermute | solution.py:106
  126.0 11.0 %collective-permute-start.6 = (bf16[384,768]{1,0:T(8,128)(2,1)S(1)}, bf16[384,768]{1,0:T(8,128)(2,1)S(1)}, u32[]{:S(2)}, u32[]{:S(2)}) collective-permute-start(bf16[384,768]{1,0:T(8,128)(2,1)S(1)} %collective-permute-done.5), channel_id=1, source_target_pairs={{0,28},{4,0},{8,4},{12,8},{16,12},{20,16},{24,20},{28,24},{1,29},{... | collective-permute-start | bytes 1769480 | tf_op jit(solution)/shard_map/ppermute | solution.py:108
  145.6 19.4 %all-to-all-start = ((bf16[256,3,4,192]{0,3,1,2:T(8,128)(2,1)}), bf16[256,3,4,192]{0,3,1,2:T(8,128)(2,1)S(1)}, u32[]{:S(2)}, u32[]{:S(2)}) async-start(bf16[256,3,4,192]{0,3,1,2:T(8,128)(2,1)} %copy.70), calls=%async_computation | async-start | bytes 2359296 | tf_op jit(solution)/shard_map/all_to_all | solution.py:135
  195.4 36.1 %all-to-all-start.1 = ((bf16[4,256,192]{1,2,0:T(8,128)(2,1)}), bf16[4,256,192]{1,2,0:T(8,128)(2,1)S(1)}, u32[]{:S(2)}, u32[]{:S(2)}) async-start(bf16[4,256,192]{1,2,0:T(8,128)(2,1)} %copy.74), calls=%async_computation.1 | async-start | bytes 786432 | tf_op jit(solution)/shard_map/all_to_all | solution.py:170
  198.9 267.8 %reduce-scatter.29.cloned.1.call-start = ((), (), s32[]{:S(2)}) async-start(), calls=%async_computation.22 | async-start | bytes 1474560
  333.6 135.1 %reduce-scatter.23.cloned.1.call-start = ((), (), s32[]{:S(2)}) async-start(), calls=%async_computation.19 | async-start | bytes 5898240 | tf_op jit(solution)/shard_map/reduce_scatter | solution.py:293
  342.8 14.8 %all-to-all-start.2 = ((bf16[256,4,192]{0,2,1:T(8,128)(2,1)}), bf16[256,4,192]{0,2,1:T(8,128)(2,1)S(1)}, u32[]{:S(2)}, u32[]{:S(2)}) async-start(bf16[256,4,192]{0,2,1:T(8,128)(2,1)} %bitcast.16), calls=%async_computation.2 | async-start | bytes 786432 | tf_op jit(solution)/shard_map/all_to_all | solution.py:205
  346.3 123.1 %reduce-scatter.31.cloned.1.call-start = ((), (), s32[]{:S(2)}) async-start(), calls=%async_computation.23 | async-start | bytes 5898240
  411.0 37.5 %all-to-all-start.3 = ((bf16[1024,3,1,192]{3,1,2,0:T(4,128)(2,1)}), bf16[1024,3,1,192]{3,1,2,0:T(4,128)(2,1)S(1)}, u32[]{:S(2)}, u32[]{:S(2)}) async-start(bf16[1024,3,1,192]{3,1,2,0:T(4,128)(2,1)} %copy.80), calls=%async_computation.3 | async-start | bytes 4194304 | tf_op jit(solution)/shard_map/all_to_all | solution.py:247
  414.6 115.2 %reduce-scatter.27.cloned.1.call-start = ((), (), s32[]{:S(2)}) async-start(), calls=%async_computation.21 | async-start | bytes 8847360
  466.7 129.2 %reduce-scatter.19.cloned.1.call-start = ((), (), s32[]{:S(2)}) async-start(), calls=%async_computation.17 | async-start | bytes 663552 | tf_op jit(solution)/shard_map/reduce_scatter | solution.py:303
  468.7 193.9 %reduce-scatter.25.cloned.1.call-start = ((), (), s32[]{:S(2)}) async-start(), calls=%async_computation.20 | async-start | bytes 1327104 | tf_op jit(solution)/shard_map/reduce_scatter | solution.py:305
  469.2 265.4 %reduce-scatter.21.cloned.1.call-start = ((), (), s32[]{:S(2)}) async-start(), calls=%async_computation.18 | async-start | bytes 2654208 | tf_op jit(solution)/shard_map/reduce_scatter | solution.py:304
  473.4 343.4 %reduce-scatter.17.cloned.1.call-start = ((), (), s32[]{:S(2)}) async-start(), calls=%async_computation.16 | async-start | bytes 3981312 | tf_op jit(solution)/shard_map/reduce_scatter | solution.py:302
  (44 other events, 422.1 us)
Sparse Core Ops, SparseCore 0:
  10.2 97.6 all-gather.4
  110.1 79.6 all-gather.8
  191.9 39.5 all-gather.6
  233.6 78.6 all-gather.10
  333.7 27.2 reduce-scatter.28
  363.6 45.1 reduce-scatter.22
  411.3 55.6 reduce-scatter.30
  469.7 60.0 reduce-scatter.26
  533.7 62.0 reduce-scatter.18
  599.4 63.1 reduce-scatter.24
  666.5 68.1 reduce-scatter.20
  738.6 78.2 reduce-scatter.16
